TPU v7x, 256 devices: a whole 4x4x8 slice. The times are simulated.
256 devices in a mesh: seq: 32 (over y, x, core), tp: 8 (over z).
Axes of the slice: x: 4, y: 4, z: 8, core: 2. Of those that a mesh axis runs over, the one named last changes fastest.
Arguments:
- queries: bfloat16 [32, 64, 4096], P('seq', None, 'tp'), may hold values from -8 to 8
- draft_kv: bfloat16 [32, 64, 8, 128], P('seq', None, 'tp'), may hold values from -12.5 to 12.5
- cache_kv: bfloat16 [8, 16384, 8, 128], P(None, 'seq', 'tp'), may hold values from -10 to 10
- cache_len: int32 [8], replicated, may hold values from 4096 to 16384
- group_of: int32 [32], replicated, may hold values from 0 to 7, as said below
- parents: int32 [32, 64], P('seq'), may hold values from 0 to 62, as said below
- sink_logit: float32 [64], P('tp'), may hold values from 4 to 20
- w_out: bfloat16 [4096, 2880], P('tp'), may hold values from -0.09375 to 0.09375
- hidden_in: bfloat16 [2048, 2880], P('seq', 'tp'), may hold values from -3 to 3
- norm_gain: float32 [2880], replicated, may hold values from 0.5 to 1.5
- routes: int32 [2048, 4], P('seq'), may hold values from 0 to 31, all different within a row; in each aligned block of 64 rows (0 to 63, 64 to 127, ...) at most 16 rows name the same one
- route_weight: float32 [2048, 4], P('seq'), may hold values from 0.1 to 1
- w_gate_up: bfloat16 [32, 2, 2880, 2880], P('seq', None, None, 'tp'), may hold values from -0.109375 to 0.109375
- w_down: bfloat16 [32, 2880, 2880], P('seq', 'tp'), may hold values from -0.109375 to 0.109375
- accepted_idx: int32 [32, 16], P('seq'), may hold values from 0 to 45, as said below
- accepted_len: int32 [32], P('seq'), may hold values from 1 to 16, as said below
- tail_slot: int32 [32], replicated, may hold values from 0 to 31, each once
Outputs:
- out_hidden: bfloat16 [2048, 2880], P('seq', 'tp')
- new_tail: bfloat16 [32, 16, 8, 128], P('seq', None, 'tp')
Inputs may be any that keep to these rules, and one draw needn't show every extreme that they name: `parents`: node 0 of every tree is its root and its own parent; every other node's parent is one of the three nodes before it. `accepted_idx`: row r lists the first 16 nodes of a path from the root of request r's tree down to one of its last four nodes, root first. `accepted_len`: each request accepts one or more nodes. `group_of`: every prompt group has exactly 4 requests. `routes`: the 4 experts of a token differ; at most 16 of one device's rows (one aligned block of 64 tokens) name one expert.
All inputs are finite; a program needn't handle non-finite values.
Results may differ from a plain program's by a relative error of at most 0.025.
Values may be sent and summed in bfloat16 or wider, within the bound.
A program may use at most 128 MiB of HBM per device.

v0:
```python
import jax
import jax.numpy as jnp
from jax import lax
from jax.sharding import PartitionSpec as P

HQ = 64
KVH = 8
HD = 64


def ancestry(parents):
    tree_len = parents.shape[1]
    node_ids = jnp.arange(tree_len, dtype=jnp.int32)
    linked = (parents[:, :, None] == node_ids[None, None, :]) | (
        node_ids[:, None] == node_ids[None, :]
    )[None]
    reachable = linked.astype(jnp.float32)
    for repeat in range((tree_len - 1).bit_length()):
        reachable = jnp.minimum(
            jnp.einsum("rij,rjk->rik", reachable, reachable, precision=lax.Precision.HIGHEST), 1.0
        )
    return reachable


def cache_block(block_queries, block_groups, cache_kv, cache_len, positions):
    block_rows, tree_len, head_cols = block_queries.shape
    kv_dev = cache_kv.shape[2]
    grouped = block_queries.reshape(block_rows, tree_len, kv_dev, HQ // KVH, HD)
    picked = jnp.take(cache_kv, block_groups, axis=0)
    cache_keys = picked[..., :HD]
    cache_values = picked[..., HD:]
    scores = (
        jnp.einsum("rtkqd,rckd->rkqtc", grouped, cache_keys, preferred_element_type=jnp.float32)
        * 0.125
    )
    lengths = jnp.take(cache_len, block_groups)
    usable = (positions[None, :] < lengths[:, None])[:, None, None, None, :]
    masked = jnp.where(usable, scores, -1e30)
    shard_max = jnp.max(masked, axis=-1)
    weights = jnp.where(usable, jnp.exp(masked - shard_max[..., None]), 0.0)
    shard_sum = jnp.sum(weights, axis=-1)
    shard_out = jnp.einsum(
        "rkqtc,rckd->rkqtd",
        weights.astype(jnp.bfloat16),
        cache_values,
        preferred_element_type=jnp.float32,
    )
    shard_out = (shard_out / jnp.maximum(shard_sum, 1.0)[..., None]).astype(jnp.bfloat16)
    out_rows = shard_out.transpose(0, 3, 1, 2, 4).reshape(block_rows, tree_len, head_cols)
    max_rows = shard_max.transpose(0, 3, 1, 2).reshape(block_rows, tree_len, -1)
    sum_rows = shard_sum.transpose(0, 3, 1, 2).reshape(block_rows, tree_len, -1)
    return (out_rows, max_rows, sum_rows)


def expert_rows(arrived, w_gate_up, w_down):
    exp_dev = w_gate_up.shape[0]
    sources = arrived.shape[0] // exp_dev
    grouped = arrived.reshape(sources, exp_dev, arrived.shape[1], arrived.shape[2])
    gate_proj = jnp.einsum(
        "sexd,edf->sexf", grouped, w_gate_up[:, 0], preferred_element_type=jnp.float32
    )
    upward = jnp.einsum(
        "sexd,edf->sexf", grouped, w_gate_up[:, 1], preferred_element_type=jnp.float32
    )
    active = (gate_proj * jax.nn.sigmoid(1.702 * gate_proj) * (upward + 1.0)).astype(jnp.bfloat16)
    down_part = jnp.einsum("sexf,efd->sexd", active, w_down, preferred_element_type=jnp.float32)
    return down_part.reshape(arrived.shape[0], arrived.shape[1], -1)


def shards(
    queries,
    draft_kv,
    cache_kv,
    cache_len,
    group_of,
    parents,
    sink_logit,
    w_out,
    hidden_in,
    norm_gain,
    routes,
    route_weight,
    w_gate_up,
    w_down,
    accepted_idx,
    accepted_len,
    tail_slot,
):
    seq_count = lax.axis_size("seq")
    req_dev, tree_len, head_cols = queries.shape
    kv_dev = cache_kv.shape[2]
    per_kv = HQ // KVH
    heads_dev = kv_dev * per_kv
    shard_len = cache_kv.shape[1]
    positions = lax.axis_index("seq") * shard_len + jnp.arange(shard_len, dtype=jnp.int32)
    every_query = lax.all_gather(queries, "seq", axis=0, tiled=True)
    requests_all = every_query.shape[0]
    block_count = requests_all // 8
    stacked = (
        every_query.reshape(block_count, 8, tree_len, head_cols),
        group_of.reshape(block_count, 8),
    )
    shard_out, shard_max, shard_sum = lax.map(
        lambda blocks: cache_block(blocks[0], blocks[1], cache_kv, cache_len, positions), stacked
    )
    shard_out = shard_out.reshape(seq_count, req_dev, tree_len, head_cols)
    shard_max = shard_max.reshape(seq_count, req_dev, tree_len, heads_dev)
    shard_sum = shard_sum.reshape(seq_count, req_dev, tree_len, heads_dev)
    came_out = lax.all_to_all(shard_out, "seq", split_axis=0, concat_axis=0, tiled=True)
    came_max, came_sum = (
        lax.all_to_all(shard_max, "seq", split_axis=0, concat_axis=0, tiled=True),
        lax.all_to_all(shard_sum, "seq", split_axis=0, concat_axis=0, tiled=True),
    )
    reachable = ancestry(parents)
    own_heads = queries.reshape(req_dev, tree_len, kv_dev, per_kv, HD)
    draft_keys = draft_kv[..., :HD]
    draft_values = draft_kv[..., HD:]
    tree_scores = (
        jnp.einsum("rtkqd,rukd->rkqtu", own_heads, draft_keys, preferred_element_type=jnp.float32)
        * 0.125
    )
    allowed = (reachable > 0.5)[:, None, None, :, :]
    tree_masked = jnp.where(allowed, tree_scores, -1e30)
    tree_max = jnp.max(tree_masked, axis=-1)
    tree_weight = jnp.where(allowed, jnp.exp(tree_masked - tree_max[..., None]), 0.0)
    tree_sum = jnp.sum(tree_weight, axis=-1)
    tree_num = jnp.einsum(
        "rkqtu,rukd->rkqtd",
        tree_weight.astype(jnp.bfloat16),
        draft_values,
        preferred_element_type=jnp.float32,
    )
    tree_max = tree_max.transpose(0, 3, 1, 2).reshape(req_dev, tree_len, heads_dev)
    tree_sum = tree_sum.transpose(0, 3, 1, 2).reshape(req_dev, tree_len, heads_dev)
    tree_num = tree_num.transpose(0, 3, 1, 2, 4).reshape(req_dev, tree_len, heads_dev, HD)
    sink_rows = sink_logit[None, None, :]
    ceiling = jnp.maximum(jnp.maximum(jnp.max(came_max, axis=0), tree_max), sink_rows)
    shard_scale = came_sum * jnp.exp(came_max - ceiling[None])
    tree_scale = jnp.exp(tree_max - ceiling)
    denominator = (
        jnp.sum(shard_scale, axis=0) + tree_scale * tree_sum + jnp.exp(sink_rows - ceiling)
    )
    weighted = jnp.sum(
        shard_scale[..., None]
        * came_out.reshape(seq_count, req_dev, tree_len, heads_dev, HD).astype(jnp.float32),
        axis=0,
    )
    numerator = weighted + tree_scale[..., None] * tree_num
    attention = (
        (numerator / denominator[..., None])
        .reshape(req_dev * tree_len, heads_dev * HD)
        .astype(jnp.bfloat16)
    )
    projected = jnp.dot(attention, w_out, preferred_element_type=jnp.float32)
    width_dev = hidden_in.shape[1]
    tp_index = lax.axis_index("tp")
    summed = lax.psum(projected, "tp")
    resid_full = lax.all_gather(hidden_in, "tp", axis=1, tiled=True)
    stream = (resid_full.astype(jnp.float32) + summed).astype(jnp.bfloat16)
    stream_f = stream.astype(jnp.float32)
    inv_scale = lax.rsqrt(jnp.mean(stream_f * stream_f, axis=-1, keepdims=True) + 1e-05)
    normed_full = (stream_f * inv_scale * norm_gain[None, :]).astype(jnp.bfloat16)
    stream_cols = lax.dynamic_slice_in_dim(stream, tp_index * width_dev, width_dev, 1)
    tok_dev = routes.shape[0]
    top_count = routes.shape[1]
    exp_dev = w_gate_up.shape[0]
    experts_all = seq_count * exp_dev
    capacity = 2 * tok_dev * top_count // experts_all
    flat_routes = routes.reshape(-1)
    onehot = (flat_routes[:, None] == jnp.arange(experts_all, dtype=jnp.int32)[None, :]).astype(
        jnp.int32
    )
    position = jnp.sum((jnp.cumsum(onehot, axis=0) - onehot) * onehot, axis=1)
    slot_ids = flat_routes * capacity + position
    buckets = jnp.arange(experts_all * capacity, dtype=jnp.int32)
    placing = jnp.sum(
        (slot_ids.reshape(tok_dev, top_count)[None, :, :] == buckets[:, None, None]).astype(
            jnp.int32
        ),
        axis=2,
    ).astype(jnp.bfloat16)
    dispatched = (
        jnp.dot(placing, normed_full, preferred_element_type=jnp.float32)
        .astype(jnp.bfloat16)
        .reshape(experts_all, capacity, -1)
    )
    down_part = expert_rows(
        lax.all_to_all(dispatched, "seq", split_axis=0, concat_axis=0, tiled=True),
        w_gate_up,
        w_down,
    )
    expert_out = lax.psum_scatter(
        down_part.astype(jnp.bfloat16), "tp", scatter_dimension=2, tiled=True
    )
    returned = lax.all_to_all(expert_out, "seq", split_axis=0, concat_axis=0, tiled=True)
    gathered_rows = jnp.take(
        returned.reshape(experts_all * capacity, -1), slot_ids, axis=0
    ).reshape(tok_dev, top_count, -1)
    mixture = jnp.sum(route_weight[:, :, None] * gathered_rows.astype(jnp.float32), axis=1)
    out_hidden = (stream_cols.astype(jnp.float32) + mixture).astype(jnp.bfloat16)
    blk_len = accepted_idx.shape[1]
    chosen = draft_kv[jnp.arange(req_dev, dtype=jnp.int32)[:, None], accepted_idx]
    kept_rows = jnp.arange(blk_len, dtype=jnp.int32)[None, :] < accepted_len[:, None]
    picked_rows = jnp.where(kept_rows[:, :, None, None], chosen, jnp.zeros_like(chosen))
    everyone = lax.all_gather(picked_rows, "seq", axis=0, tiled=True)
    my_slots = lax.axis_index("seq") * req_dev + jnp.arange(req_dev, dtype=jnp.int32)
    selector = (tail_slot[None, :] == my_slots[:, None]).astype(jnp.bfloat16)
    new_tail = jnp.dot(
        selector, everyone.reshape(everyone.shape[0], -1), preferred_element_type=jnp.float32
    ).astype(jnp.bfloat16)
    new_tail = new_tail.reshape(req_dev, blk_len, kv_dev, -1)
    return (out_hidden, new_tail)


def solution(mesh):
    in_specs = (
        P("seq", None, "tp"),
        P("seq", None, "tp", None),
        P(None, "seq", "tp", None),
        P(),
        P(),
        P("seq", None),
        P("tp"),
        P("tp", None),
        P("seq", "tp"),
        P(),
        P("seq", None),
        P("seq", None),
        P("seq", None, None, "tp"),
        P("seq", "tp", None),
        P("seq", None),
        P("seq"),
        P(),
    )
    out_specs = (P("seq", "tp"), P("seq", None, "tp", None))
    return jax.shard_map(shards, mesh=mesh, in_specs=in_specs, out_specs=out_specs, check_vma=False)
```

profile of v0, /device:TPU:1, one launch (start us, length us, event | category | flops | bytes accessed | tf_op | source)
XLA Modules:
  0.0 533.3 jit_solution(3878875501359007208)
XLA Ops:
  10.3 53.3 %all-gather.3.cloned.1.call-done = bf16[32,64,512]{2,1,0:T(8,128)(2,1)} async-done(((bf16[1,64,512]{2,1,0:T(8,128)(2,1)}), bf16[32,64,512]{2,1,0:T(8,128)(2,1)}) %all-gather.3.cloned.1.call-update) | async-done | bytes 2097168 | tf_op jit(solution)/shard_map/all_gather | solution.py:96
  63.7 97.3 %while.15 = (s32[]{:T(128)}, bf16[4,8,64,512]{3,2,1,0:T(8,128)(2,1)}, f32[4,8,64,8]{2,3,1,0:T(8,128)}, f32[4,8,64,8]{2,3,1,0:T(8,128)}, s32[4,8]{1,0:T(4,128)S(1...) while((s32[]{:T(128)}, ...), condition=%wide.region_3.4_spmd.clone, body=%wide.region_0.3_spmd.clone.sunk | while | flops 565184128 | bytes 43791872 | solution.py:103
  65.0 2.9 gather_fusion.1
  75.3 2.7 bitcast_reduce_fusion.3
  89.4 2.9 gather_fusion.1
  99.6 2.7 bitcast_reduce_fusion.3
  113.7 2.9 gather_fusion.1
  124.0 2.7 bitcast_reduce_fusion.3
  138.0 2.9 gather_fusion.1
  148.3 2.7 bitcast_reduce_fusion.3
  162.7 5.1 all-to-all-start.1
  170.4 4.7 all-to-all-done.1
  175.1 3.9 all-to-all-start
  180.8 5.6 %all-to-all-done = f32[32,1,512]{2,1,0:T(1,128)S(1)} async-done(((f32[32,1,512]{2,1,0:T(1,128)}), f32[32,1,512]{2,1,0:T(1,128)S(1)}, u32[]{:S(2)}, u32[]{:S(2)}) %all-to-all-start) | async-done | bytes 65568 | tf_op jit(solution)/shard_map/all_to_all | solution.py:112
  186.4 4.7 all-to-all-start.2
  193.3 23.3 %all-gather = bf16[8,360,64]{1,2,0:T(8,128)(2,1)S(1)} all-gather(bf16[1,360,64]{1,2,0:T(8,128)(2,1)} %bitcast.318), channel_id=1, replica_groups=mesh['seq'=32,'tp'=8] {'tp'}, dimensions={0}, use_global_device_ids=true | all-gather | bytes 414720 | tf_op jit(solution)/shard_map/all_gather | solution.py:158
  227.4 5.9 %mul.135 = f32[32,64,8,64]{3,2,1,0:T(8,128)} broadcast(f32[32,64,8]{2,1,0:T(8,128)} %copy.92), dimensions={0,1,2} | broadcast | bytes 4259840 | tf_op jit(solution)/shard_map/mul | solution.py:144
  233.4 7.5 %mul.136 = f32[32,1,64,512]{3,2,1,0:T(8,128)} reshape(f32[32,64,8,64]{3,2,1,0:T(8,128)} %mul.135) | data formatting | bytes 8388608 | tf_op jit(solution)/shard_map/mul | solution.py:144
  240.9 3.6 multiply_reduce_fusion
  247.8 72.6 %all-reduce.3.cloned.1.call-done = f32[64,2880]{1,0:T(8,128)} async-done(((f32[64,2880]{1,0:T(8,128)}), f32[64,2880]{1,0:T(8,128)}) %all-reduce.3.cloned.1.call-update) | async-done | bytes 737296 | tf_op jit(solution)/shard_map/psum | solution.py:157
  325.4 4.6 copy.103
  329.9 50.3 %all_to_all.25 = bf16[32,16,2880]{2,1,0:T(8,128)(2,1)S(1)} all-to-all(bf16[32,16,2880]{2,1,0:T(8,128)(2,1)} %bitcast.309), channel_id=1, replica_groups=mesh['seq'=32,'tp'=8] {'seq'}, dimensions={0} | all-to-all | bytes 5898240 | tf_op jit(solution)/shard_map/all_to_all | solution.py:188
  381.9 4.2 fusion.27
  386.1 8.5 %convolution_convert_fusion = bf16[32,16,2880]{2,1,0:T(8,128)(2,1)} fusion(bf16[1,360,2880]{2,1,0:T(8,128)(2,1)} %param.32, bf16[32,16,2880]{2,1,0:T(8,128)(2,1)} %copy-done.2, bf16[1,2,2880,360]{2,3,1,0:T(8,128)(2,1)} %param.31, f32[32,1,16,360]{3,2,0,1:T(8,128)} %fusion.27), kind=kOutput, calls=%fused_computation.40 | convolution fusion | flops 2126315520 | bytes 10989568 | tf_op jit(solution)/shard_map/sexf,efd->sexd/dot_general | solution.py:66
  394.6 21.4 %copy.108 = bf16[32,16,2880]{1,0,2:T(8,128)(2,1)} copy(bf16[32,16,2880]{2,1,0:T(8,128)(2,1)} %convolution_convert_fusion) | data formatting | bytes 5898240
  416.0 39.5 %reshape.749 = bf16[2880,512]{1,0:T(8,128)(2,1)} reshape(bf16[2880,32,16]{2,1,0:T(8,128)(2,1)} %bitcast.306) | data formatting | bytes 5898240
  457.1 22.6 %all_gather.11 = bf16[32,16,1,128]{3,1,2,0:T(8,128)(2,1)S(1)} all-gather(bf16[1,16,1,128]{3,1,2,0:T(8,128)(2,1)S(1)} %bitcast_select_fusion.2), channel_id=1, replica_groups=mesh['seq'=32,'tp'=8] {'seq'}, dimensions={0}, use_global_device_ids=true | all-gather | bytes 135168 | tf_op jit(solution)/shard_map/all_gather | solution.py:205
  479.9 12.3 %reduce-scatter.4.cloned.1.call-done = bf16[360,512]{1,0:T(8,128)(2,1)} async-done(((bf16[2880,512]{1,0:T(8,128)(2,1)}), bf16[360,512]{1,0:T(8,128)(2,1)}) %reduce-scatter.4.cloned.1.call-update) | async-done | bytes 368656
  492.2 4.4 reshape.750
  496.5 5.0 copy.109
  501.6 11.1 %all-to-all-start.4 = ((bf16[32,16,360]{2,1,0:T(8,128)(2,1)}), bf16[32,16,360]{2,1,0:T(8,128)(2,1)S(1)}, u32[]{:S(2)}, u32[]{:S(2)}) async-start(bf16[32,16,360]{2,1,0:T(8,128)(2,1)} %copy.109), calls=%async_computation.4 | async-start | bytes 786432 | tf_op jit(solution)/shard_map/all_to_all | solution.py:195
  514.1 8.7 %all-to-all-done.4 = bf16[32,16,360]{2,1,0:T(8,128)(2,1)S(1)} async-done(((bf16[32,16,360]{2,1,0:T(8,128)(2,1)}), bf16[32,16,360]{2,1,0:T(8,128)(2,1)S(1)}, u32[]{:S(2)}, u32[]{:S(2)}) %all-to-all-start.4) | async-done | bytes 368672 | tf_op jit(solution)/shard_map/all_to_all | solution.py:195
  (194 shorter events, 113.0 us)
Async XLA Ops:
  7.2 237.3 %copy-start = (bf16[512,2880]{0,1:T(8,128)(2,1)S(1)}, bf16[512,2880]{0,1:T(8,128)(2,1)}, u32[]{:S(2)}) copy-start(bf16[512,2880]{0,1:T(8,128)(2,1)} %param.26) | copy-start | bytes 8847364
  7.2 56.5 %all-gather.3.cloned.1.call-start = ((), (), s32[]{:S(2)}) async-start(), calls=%async_computation.6 | async-start | bytes 2162688 | tf_op jit(solution)/shard_map/all_gather | solution.py:96
  63.7 115.5 %copy-start.6 = (bf16[1,64,512]{2,1,0:T(8,128)(2,1)S(1)}, bf16[1,64,512]{2,1,0:T(8,128)(2,1)}, u32[]{:S(2)}) copy-start(bf16[1,64,512]{2,1,0:T(8,128)(2,1)} %param.19) | copy-start | bytes 196612
  63.7 115.6 %copy-start.13 = (s32[64,4]{0,1:T(4,128)S(1)}, s32[64,4]{0,1:T(4,128)}, u32[]{:S(2)}) copy-start(s32[64,4]{0,1:T(4,128)} %param.29) | copy-start | bytes 3076
  78.0 3.0 copy-start.1
  102.3 3.0 copy-start.1
  126.6 3.0 copy-start.1
  150.9 3.0 copy-start.1
  161.0 30.9 %copy-start.7 = (bf16[1,64,1,128]{3,1,2,0:T(8,128)(2,1)S(1)}, bf16[1,64,1,128]{3,1,2,0:T(8,128)(2,1)}, u32[]{:S(2)}) copy-start(bf16[1,64,1,128]{3,1,2,0:T(8,128)(2,1)} %param.20) | copy-start | bytes 49156
  162.7 12.4 %all-to-all-start.1 = ((f32[32,1,512]{2,1,0:T(1,128)}), f32[32,1,512]{2,1,0:T(1,128)S(1)}, u32[]{:S(2)}, u32[]{:S(2)}) async-start(f32[32,1,512]{2,1,0:T(1,128)} %reshape.754), calls=%async_computation.1 | async-start | bytes 131072 | tf_op jit(solution)/shard_map/all_to_all | solution.py:111
  175.1 17.0 %copy-start.9 = (f32[32,1,512]{2,1,0:T(1,128)}, f32[32,1,512]{2,1,0:T(1,128)S(1)}, u32[]{:S(2)}) copy-start(f32[32,1,512]{2,1,0:T(1,128)S(1)} %all-to-all-done.1) | copy-start | bytes 196612
  175.1 11.3 %all-to-all-start = ((f32[32,1,512]{2,1,0:T(1,128)}), f32[32,1,512]{2,1,0:T(1,128)S(1)}, u32[]{:S(2)}, u32[]{:S(2)}) async-start(f32[32,1,512]{2,1,0:T(1,128)} %reshape.752), calls=%async_computation | async-start | bytes 131072 | tf_op jit(solution)/shard_map/all_to_all | solution.py:112
  186.4 4.8 copy-start.11
  186.4 54.4 %all-to-all-start.2 = ((bf16[32,1,64,512]{3,2,1,0:T(8,128)(2,1)}), bf16[32,1,64,512]{3,2,1,0:T(8,128)(2,1)}, u32[]{:S(2)}, u32[]{:S(2)}) async-start(bf16[32,1,64,512]{3,2,1,0:T(8,128)(2,1)} %bitcast.313), calls=%async_computation.2 | async-start | bytes 4194304 | tf_op jit(solution)/shard_map/all_to_all | solution.py:109
  191.2 129.2 %all-reduce.3.cloned.1.call-start = ((), (), s32[]{:S(2)}) async-start(), calls=%async_computation.7 | async-start | bytes 1507328 | tf_op jit(solution)/shard_map/psum | solution.py:157
  192.4 28.8 %copy-start.10 = (f32[32,1,512]{2,1,0:T(1,128)S(1)}, f32[32,1,512]{2,1,0:T(1,128)}, u32[]{:S(2)}) copy-start(f32[32,1,512]{2,1,0:T(1,128)} %copy-done.9) | copy-start | bytes 196612
  193.3 28.8 %copy-start.12 = (f32[32,1,512]{2,1,0:T(1,128)S(1)}, f32[32,1,512]{2,1,0:T(1,128)}, u32[]{:S(2)}) copy-start(f32[32,1,512]{2,1,0:T(1,128)} %copy-done.11) | copy-start | bytes 196612
  240.9 3.6 copy-start.4
  240.9 3.6 copy-start.5
  244.5 2.0 copy-start.16
  244.5 2.8 copy-start.15
  244.5 78.2 %copy-start.14 = (f32[2880]{0:T(1024)S(1)}, f32[2880]{0:T(1024)}, u32[]{:S(2)}) copy-start(f32[2880]{0:T(1024)} %param.28) | copy-start | bytes 34564
  246.4 245.7 %reduce-scatter.4.cloned.1.call-start = ((), (), s32[]{:S(2)}) async-start(), calls=%async_computation.8 | async-start | bytes 3317760
  321.9 0.8 copy-start.3
  380.2 1.6 copy-start.2
  455.4 0.9 copy-start.19
  455.4 1.0 copy-start.8
  455.4 24.3 %copy-start.18 = (s32[32]{0:T(128)S(1)}, s32[32]{0:T(128)}, u32[]{:S(2)}) copy-start(s32[32]{0:T(128)} %param.35) | copy-start | bytes 388
  479.8 33.0 %copy-start.17 = (f32[64,4]{0,1:T(4,128)S(1)}, f32[64,4]{0,1:T(4,128)}, u32[]{:S(2)}) copy-start(f32[64,4]{0,1:T(4,128)} %param.30) | copy-start | bytes 3076
  501.6 21.3 %all-to-all-start.4 = ((bf16[32,16,360]{2,1,0:T(8,128)(2,1)}), bf16[32,16,360]{2,1,0:T(8,128)(2,1)S(1)}, u32[]{:S(2)}, u32[]{:S(2)}) async-start(bf16[32,16,360]{2,1,0:T(8,128)(2,1)} %copy.109), calls=%async_computation.4 | async-start | bytes 786432 | tf_op jit(solution)/shard_map/all_to_all | solution.py:195
Sparse Core Ops, SparseCore 0:
  10.6 53.0 all-gather.2
  246.5 73.8 all-reduce.2
  455.6 36.5 reduce-scatter.3
where the time goes:
time: 536 us; the launch traced here: 533 us
  local copies, waits for them, and re-layouts  164 us (31%)
  waiting for transfers between devices  158 us (29%)
  blocking collectives  96.2 us (18%)
  matrix products  42.4 us (8%)
  other arithmetic  32.4 us (6%)
  starting transfers between devices  25 us (5%)
  between operations  14.9 us (3%)
    unnamed x48, local copies, waits for them, and re-layouts  77 us
    psum x1, waiting for transfers between devices, shards(): summed = lax.psum(projected, 'tp')  72.6 us
    all_gather x1, waiting for transfers between devices, shards(): every_query = lax.all_gather(queries, 'seq', axis=0, tiled=True)  53.3 us
    all_to_all x1, blocking collectives, shards(): lax.all_to_all(dispatched, 'seq', split_axis=0, concat_axis=0, tiled=True)  50.3 us
    all_gather x1, blocking collectives, shards(): resid_full = lax.all_gather(hidden_in, 'tp', axis=1, tiled=True)  23.3 us
    all_gather x1, blocking collectives, shards(): everyone = lax.all_gather(picked_rows, 'seq', axis=0, tiled=True)  22.6 us
    gather x8, local copies, waits for them, and re-layouts, cache_block(): picked = jnp.take(cache_kv, block_groups, axis=0)  20.7 us
    mul x3, local copies, waits for them, and re-layouts, shards(): shard_scale[..., None]  14.9 us
  transfers between devices with their start and end apart: 7, of which 6 were waited for; matrix products, arithmetic and copies ran while one was open for 7% of the time, Pallas kernels for 0%

commit v1 on v0

--- a/solution.py
+++ b/solution.py
@@ -155,7 +155,12 @@
     width_dev = hidden_in.shape[1]
     tp_index = lax.axis_index("tp")
     summed = lax.psum(projected, "tp")
-    resid_full = lax.all_gather(hidden_in, "tp", axis=1, tiled=True)
+    ring = [hidden_in]
+    for hop in range(7):
+        ring.append(lax.ppermute(ring[-1], "tp", [(dev, (dev + 1) % 8) for dev in range(8)]))
+    resid_full = jnp.roll(
+        jnp.concatenate(ring[::-1], axis=1), (lax.axis_index("tp") + 1) * ring[0].shape[1], axis=1
+    )
     stream = (resid_full.astype(jnp.float32) + summed).astype(jnp.bfloat16)
     stream_f = stream.astype(jnp.float32)
     inv_scale = lax.rsqrt(jnp.mean(stream_f * stream_f, axis=-1, keepdims=True) + 1e-05)

time: 536 us -> 513 us (0.957)
  blocking collectives: 96.2 us -> 72.9 us
    all_gather x1 -> x0, blocking collectives: 23.3 us -> none  [shards(): resid_full = lax.all_gather(hidden_in, 'tp', axis=1, tiled=True)]
    psum x1, waiting for transfers between devices: 72.6 us -> 51.6 us  [shards(): summed = lax.psum(projected, 'tp')]
    ppermute x0 -> x7, waiting for transfers between devices: none -> 19.1 us  [shards(): lax.ppermute(ring[-1], 'tp', [(dev, (dev + 1) % 8) for dev in range(8)])]
    unnamed x48 -> x40, local copies, waits for them, and re-layouts: 77 us -> 77 us
  transfers between devices with their start and end apart: 7 -> 14, of which waited for: 6 -> 11; matrix products, arithmetic and copies ran while one was open for 7% -> 27% of each run, Pallas kernels for 0% -> 0%
where the time goes in v1:
time: 513 us; the launch traced here: 511 us
  local copies, waits for them, and re-layouts  163 us (32%)
  waiting for transfers between devices  158 us (31%)
  blocking collectives  72.9 us (14%)
  matrix products  40.2 us (8%)
  other arithmetic  31.5 us (6%)
  starting transfers between devices  30 us (6%)
  between operations  14.8 us (3%)
    unnamed x40, local copies, waits for them, and re-layouts  77 us
    all_gather x1, waiting for transfers between devices, shards(): every_query = lax.all_gather(queries, 'seq', axis=0, tiled=True)  52.5 us
    psum x1, waiting for transfers between devices, shards(): summed = lax.psum(projected, 'tp')  51.6 us
    all_to_all x1, blocking collectives, shards(): lax.all_to_all(dispatched, 'seq', split_axis=0, concat_axis=0, tiled=True)  50.3 us
    all_gather x1, blocking collectives, shards(): everyone = lax.all_gather(picked_rows, 'seq', axis=0, tiled=True)  22.6 us
    gather x8, local copies, waits for them, and re-layouts, cache_block(): picked = jnp.take(cache_kv, block_groups, axis=0)  20.7 us
    ppermute x7, waiting for transfers between devices, shards(): lax.ppermute(ring[-1], 'tp', [(dev, (dev + 1) % 8) for dev in range(8)])  19.1 us
    mul x3, local copies, waits for them, and re-layouts, shards(): shard_scale[..., None]  15.8 us
  transfers between devices with their start and end apart: 14, of which 11 were waited for; matrix products, arithmetic and copies ran while one was open for 27% of the time, Pallas kernels for 0%

profile of v1, /device:TPU:1, one launch (start us, length us, event | category | flops | bytes accessed | tf_op | source)
XLA Modules:
  0.0 510.7 jit_solution(6322982661219075779)
XLA Ops:
  11.2 52.5 %all-gather.2.cloned.1.call-done = bf16[32,64,512]{2,1,0:T(8,128)(2,1)} async-done(((bf16[1,64,512]{2,1,0:T(8,128)(2,1)}), bf16[32,64,512]{2,1,0:T(8,128)(2,1)}) %all-gather.2.cloned.1.call-update) | async-done | bytes 2097168 | tf_op jit(solution)/shard_map/all_gather | solution.py:96
  63.7 97.3 %while.15 = (s32[]{:T(128)}, bf16[4,8,64,512]{3,2,1,0:T(8,128)(2,1)}, f32[4,8,64,8]{2,3,1,0:T(8,128)}, f32[4,8,64,8]{2,3,1,0:T(8,128)}, s32[4,8]{1,0:T(4,128)S(1...) while((s32[]{:T(128)}, ...), condition=%wide.region_3.4_spmd.clone, body=%wide.region_0.3_spmd.clone.sunk | while | flops 565184128 | bytes 43791872 | solution.py:103
  65.0 2.9 gather_fusion.1
  89.4 2.9 gather_fusion.1
  113.7 2.9 gather_fusion.1
  138.0 2.9 gather_fusion.1
  162.7 5.1 %all-to-all-start.1 = ((f32[32,1,512]{2,1,0:T(1,128)}), f32[32,1,512]{2,1,0:T(1,128)S(1)}, u32[]{:S(2)}, u32[]{:S(2)}) async-start(f32[32,1,512]{2,1,0:T(1,128)} %reshape.751), calls=%async_computation.1 | async-start | bytes 131072 | tf_op jit(solution)/shard_map/all_to_all | solution.py:111
  169.7 5.5 %all-to-all-done.1 = f32[32,1,512]{2,1,0:T(1,128)S(1)} async-done(((f32[32,1,512]{2,1,0:T(1,128)}), f32[32,1,512]{2,1,0:T(1,128)S(1)}, u32[]{:S(2)}, u32[]{:S(2)}) %all-to-all-start.1) | async-done | bytes 65568 | tf_op jit(solution)/shard_map/all_to_all | solution.py:111
  175.1 3.9 all-to-all-start
  179.2 7.3 %all-to-all-done = f32[32,1,512]{2,1,0:T(1,128)S(1)} async-done(((f32[32,1,512]{2,1,0:T(1,128)}), f32[32,1,512]{2,1,0:T(1,128)S(1)}, u32[]{:S(2)}, u32[]{:S(2)}) %all-to-all-start) | async-done | bytes 65568 | tf_op jit(solution)/shard_map/all_to_all | solution.py:112
  186.4 4.9 all-to-all-start.2
  195.3 2.7 collective-permute-done.1
  206.0 5.9 %mul.139 = f32[32,64,8,64]{3,2,1,0:T(8,128)} broadcast(f32[32,64,8]{2,1,0:T(8,128)} %copy.87), dimensions={0,1,2} | broadcast | bytes 4259840 | tf_op jit(solution)/shard_map/mul | solution.py:144
  212.0 7.5 %mul.140 = f32[32,1,64,512]{3,2,1,0:T(8,128)} reshape(f32[32,64,8,64]{3,2,1,0:T(8,128)} %mul.139) | data formatting | bytes 8388608 | tf_op jit(solution)/shard_map/mul | solution.py:144
  219.5 3.6 multiply_reduce_fusion
  227.1 3.1 collective-permute-done.3
  230.5 3.9 collective-permute-done.4
  234.4 4.2 collective-permute-done.5
  238.8 5.1 %collective-permute-done.6 = bf16[64,360]{1,0:T(8,128)(2,1)S(1)} collective-permute-done((bf16[64,360]{1,0:T(8,128)(2,1)S(1)}, bf16[64,360]{1,0:T(8,128)(2,1)S(1)}, u32[]{:S(2)}, u32[]{:S(2)}) %collective-permute-start.6) | collective-permute-done | bytes 46112 | tf_op jit(solution)/shard_map/ppermute | solution.py:160
  246.1 51.6 %all-reduce.3.cloned.1.call-done = f32[64,2880]{1,0:T(8,128)} async-done(((f32[64,2880]{1,0:T(8,128)}), f32[64,2880]{1,0:T(8,128)}) %all-reduce.3.cloned.1.call-update) | async-done | bytes 737296 | tf_op jit(solution)/shard_map/psum | solution.py:157
  302.7 4.6 copy.98
  307.2 50.3 %all_to_all.25 = bf16[32,16,2880]{2,1,0:T(8,128)(2,1)S(1)} all-to-all(bf16[32,16,2880]{2,1,0:T(8,128)(2,1)} %bitcast.299), channel_id=1, replica_groups=mesh['seq'=32,'tp'=8] {'seq'}, dimensions={0} | all-to-all | bytes 5898240 | tf_op jit(solution)/shard_map/all_to_all | solution.py:193
  359.1 4.2 fusion.27
  363.4 8.5 %convolution_convert_fusion = bf16[32,16,2880]{2,1,0:T(8,128)(2,1)} fusion(bf16[1,360,2880]{2,1,0:T(8,128)(2,1)} %param.32, bf16[32,16,2880]{2,1,0:T(8,128)(2,1)} %copy-done.2, bf16[1,2,2880,360]{2,3,1,0:T(8,128)(2,1)} %param.31, f32[32,1,16,360]{3,2,0,1:T(8,128)} %fusion.27), kind=kOutput, calls=%fused_computation.40 | convolution fusion | flops 2126315520 | bytes 10989568 | tf_op jit(solution)/shard_map/sexf,efd->sexd/dot_general | solution.py:66
  371.9 21.4 %copy.103 = bf16[32,16,2880]{1,0,2:T(8,128)(2,1)} copy(bf16[32,16,2880]{2,1,0:T(8,128)(2,1)} %convolution_convert_fusion) | data formatting | bytes 5898240
  393.2 39.5 %reshape.746 = bf16[2880,512]{1,0:T(8,128)(2,1)} reshape(bf16[2880,32,16]{2,1,0:T(8,128)(2,1)} %bitcast.296) | data formatting | bytes 5898240
  434.4 22.6 %all_gather.7 = bf16[32,16,1,128]{3,1,2,0:T(8,128)(2,1)S(1)} all-gather(bf16[1,16,1,128]{3,1,2,0:T(8,128)(2,1)S(1)} %bitcast_select_fusion.2), channel_id=1, replica_groups=mesh['seq'=32,'tp'=8] {'seq'}, dimensions={0}, use_global_device_ids=true | all-gather | bytes 135168 | tf_op jit(solution)/shard_map/all_gather | solution.py:210
  457.1 12.5 %reduce-scatter.4.cloned.1.call-done = bf16[360,512]{1,0:T(8,128)(2,1)} async-done(((bf16[2880,512]{1,0:T(8,128)(2,1)}), bf16[360,512]{1,0:T(8,128)(2,1)}) %reduce-scatter.4.cloned.1.call-update) | async-done | bytes 368656
  469.6 4.4 reshape.747
  474.0 5.0 copy.104
  479.0 11.0 %all-to-all-start.4 = ((bf16[32,16,360]{2,1,0:T(8,128)(2,1)}), bf16[32,16,360]{2,1,0:T(8,128)(2,1)S(1)}, u32[]{:S(2)}, u32[]{:S(2)}) async-start(bf16[32,16,360]{2,1,0:T(8,128)(2,1)} %copy.104), calls=%async_computation.4 | async-start | bytes 786432 | tf_op jit(solution)/shard_map/all_to_all | solution.py:200
  491.5 8.7 %all-to-all-done.4 = bf16[32,16,360]{2,1,0:T(8,128)(2,1)S(1)} async-done(((bf16[32,16,360]{2,1,0:T(8,128)(2,1)}), bf16[32,16,360]{2,1,0:T(8,128)(2,1)S(1)}, u32[]{:S(2)}, u32[]{:S(2)}) %all-to-all-start.4) | async-done | bytes 368672 | tf_op jit(solution)/shard_map/all_to_all | solution.py:200
  (198 shorter events, 124.6 us)
Async XLA Ops:
  7.2 215.9 %copy-start = (bf16[512,2880]{0,1:T(8,128)(2,1)S(1)}, bf16[512,2880]{0,1:T(8,128)(2,1)}, u32[]{:S(2)}) copy-start(bf16[512,2880]{0,1:T(8,128)(2,1)} %param.26) | copy-start | bytes 8847364
  7.2 56.5 %all-gather.2.cloned.1.call-start = ((), (), s32[]{:S(2)}) async-start(), calls=%async_computation.6 | async-start | bytes 2162688 | tf_op jit(solution)/shard_map/all_gather | solution.py:96
  7.9 184.9 %collective-permute-start = (bf16[64,360]{1,0:T(8,128)(2,1)}, bf16[64,360]{1,0:T(8,128)(2,1)}, u32[]{:S(2)}, u32[]{:S(2)}) collective-permute-start(bf16[64,360]{1,0:T(8,128)(2,1)} %param.27), channel_id=1, source_target_pairs={{0,1},{1,2},{2,3},{3,4},{4,5},{5,6},{6,7},{7,0},{8,9},{9,10},{10,1... | collective-permute-start | bytes 138248 | tf_op jit(solution)/shard_map/ppermute | solution.py:160
  63.7 104.1 %copy-start.14 = (s32[1,64]{1,0:T(1,128)S(1)}, s32[1,64]{1,0:T(1,128)}, u32[]{:S(2)}) copy-start(s32[1,64]{1,0:T(1,128)} %param.24) | copy-start | bytes 772
  78.0 3.0 copy-start.1
  102.3 3.0 copy-start.1
  126.6 3.0 copy-start.1
  150.9 3.0 copy-start.1
  161.0 30.6 %copy-start.5 = (bf16[1,64,512]{2,1,0:T(8,128)(2,1)S(1)}, bf16[1,64,512]{2,1,0:T(8,128)(2,1)}, u32[]{:S(2)}) copy-start(bf16[1,64,512]{2,1,0:T(8,128)(2,1)} %param.19) | copy-start | bytes 196612
  161.0 31.3 %copy-start.6 = (bf16[1,64,1,128]{3,1,2,0:T(8,128)(2,1)S(1)}, bf16[1,64,1,128]{3,1,2,0:T(8,128)(2,1)}, u32[]{:S(2)}) copy-start(bf16[1,64,1,128]{3,1,2,0:T(8,128)(2,1)} %param.20) | copy-start | bytes 49156
  162.7 12.5 %all-to-all-start.1 = ((f32[32,1,512]{2,1,0:T(1,128)}), f32[32,1,512]{2,1,0:T(1,128)S(1)}, u32[]{:S(2)}, u32[]{:S(2)}) async-start(f32[32,1,512]{2,1,0:T(1,128)} %reshape.751), calls=%async_computation.1 | async-start | bytes 131072 | tf_op jit(solution)/shard_map/all_to_all | solution.py:111
  175.1 11.3 %all-to-all-start = ((f32[32,1,512]{2,1,0:T(1,128)}), f32[32,1,512]{2,1,0:T(1,128)S(1)}, u32[]{:S(2)}, u32[]{:S(2)}) async-start(f32[32,1,512]{2,1,0:T(1,128)} %reshape.749), calls=%async_computation | async-start | bytes 131072 | tf_op jit(solution)/shard_map/all_to_all | solution.py:112
  186.4 8.1 %copy-start.7 = (s32[64,4]{0,1:T(4,128)S(1)}, s32[64,4]{0,1:T(4,128)}, u32[]{:S(2)}) copy-start(s32[64,4]{0,1:T(4,128)} %param.29) | copy-start | bytes 3076
  186.4 13.9 %copy-start.12 = (f32[8]{0:T(128)S(1)}, f32[8]{0:T(128)}, u32[]{:S(2)}) copy-start(f32[8]{0:T(128)} %param.25) | copy-start | bytes 100
  186.4 33.0 %all-to-all-start.2 = ((bf16[32,1,64,512]{3,2,1,0:T(8,128)(2,1)}), bf16[32,1,64,512]{3,2,1,0:T(8,128)(2,1)}, u32[]{:S(2)}, u32[]{:S(2)}) async-start(bf16[32,1,64,512]{3,2,1,0:T(8,128)(2,1)} %bitcast.303), calls=%async_computation.2 | async-start | bytes 4194304 | tf_op jit(solution)/shard_map/all_to_all | solution.py:109
  191.3 106.4 %all-reduce.3.cloned.1.call-start = ((), (), s32[]{:S(2)}) async-start(), calls=%async_computation.7 | async-start | bytes 1507328 | tf_op jit(solution)/shard_map/psum | solution.py:157
  192.8 5.2 %collective-permute-start.1 = (bf16[64,360]{1,0:T(8,128)(2,1)}, bf16[64,360]{1,0:T(8,128)(2,1)}, u32[]{:S(2)}, u32[]{:S(2)}) collective-permute-start(bf16[64,360]{1,0:T(8,128)(2,1)} %collective-permute-done), channel_id=1, source_target_pairs={{0,1},{1,2},{2,3},{3,4},{4,5},{5,6},{6,7},{7,0},{8,9},{9,10},{10,1... | collective-permute-start | bytes 138248 | tf_op jit(solution)/shard_map/ppermute | solution.py:160
  198.0 27.7 %collective-permute-start.2 = (bf16[64,360]{1,0:T(8,128)(2,1)}, bf16[64,360]{1,0:T(8,128)(2,1)}, u32[]{:S(2)}, u32[]{:S(2)}) collective-permute-start(bf16[64,360]{1,0:T(8,128)(2,1)} %collective-permute-done.1), channel_id=1, source_target_pairs={{0,1},{1,2},{2,3},{3,4},{4,5},{5,6},{6,7},{7,0},{8,9},{9,10},{10,1... | collective-permute-start | bytes 138248 | tf_op jit(solution)/shard_map/ppermute | solution.py:160
  219.4 3.6 copy-start.4
  223.0 2.0 copy-start.10
  223.1 11.3 %copy-start.8 = (s32[64,4]{0,1:T(4,128)S(1)}, s32[64,4]{0,1:T(4,128)}, u32[]{:S(2)}) copy-start(s32[64,4]{0,1:T(4,128)} %param.29) | copy-start | bytes 3076
  225.0 75.0 %copy-start.9 = (f32[2880]{0:T(1024)S(1)}, f32[2880]{0:T(1024)}, u32[]{:S(2)}) copy-start(f32[2880]{0:T(1024)} %param.28) | copy-start | bytes 34564
  225.0 244.6 %reduce-scatter.4.cloned.1.call-start = ((), (), s32[]{:S(2)}) async-start(), calls=%async_computation.8 | async-start | bytes 3317760
  225.7 4.6 collective-permute-start.3
  230.2 4.2 collective-permute-start.4
  234.4 4.3 collective-permute-start.5
  238.6 5.3 %collective-permute-start.6 = (bf16[64,360]{1,0:T(8,128)(2,1)S(1)}, bf16[64,360]{1,0:T(8,128)(2,1)S(1)}, u32[]{:S(2)}, u32[]{:S(2)}) collective-permute-start(bf16[64,360]{1,0:T(8,128)(2,1)S(1)} %collective-permute-done.5), channel_id=1, source_target_pairs={{0,1},{1,2},{2,3},{3,4},{4,5},{5,6},{6,7},{7,0},{8,9},{9,10},{10,1... | collective-permute-start | bytes 138248 | tf_op jit(solution)/shard_map/ppermute | solution.py:160
  357.5 1.6 copy-start.2
  432.7 0.9 copy-start.15
  432.7 24.2 %copy-start.13 = (s32[32]{0:T(128)S(1)}, s32[32]{0:T(128)}, u32[]{:S(2)}) copy-start(s32[32]{0:T(128)} %param.35) | copy-start | bytes 388
  457.1 33.1 %copy-start.11 = (f32[64,4]{0,1:T(4,128)S(1)}, f32[64,4]{0,1:T(4,128)}, u32[]{:S(2)}) copy-start(f32[64,4]{0,1:T(4,128)} %param.30) | copy-start | bytes 3076
  479.0 21.2 %all-to-all-start.4 = ((bf16[32,16,360]{2,1,0:T(8,128)(2,1)}), bf16[32,16,360]{2,1,0:T(8,128)(2,1)S(1)}, u32[]{:S(2)}, u32[]{:S(2)}) async-start(bf16[32,16,360]{2,1,0:T(8,128)(2,1)} %copy.104), calls=%async_computation.4 | async-start | bytes 786432 | tf_op jit(solution)/shard_map/all_to_all | solution.py:200
  (1 other events, 0.8 us)
Sparse Core Ops, SparseCore 0:
  10.6 53.0 all-gather.1
  225.1 72.5 all-reduce.2
  432.9 36.7 reduce-scatter.3
